TPU v7x, 32 devices: a whole 2x2x4 slice. The times are simulated.
32 devices in a mesh: groups: 2 (over y), ctx: 4 (over z), tensor: 2 (over x), dp: 2 (over core).
Axes of the slice: x: 2, y: 2, z: 4, core: 2. Of those that a mesh axis runs over, the one named last changes fastest.
Arguments:
- tokens: bfloat16 [4, 1024, 1024], P(('groups', 'dp'), 'ctx', 'tensor'), parts along dimension 0
- w_qkv: bfloat16 [1024, 3, 1024], P(None, None, 'tensor')
- w_out: bfloat16 [1024, 1024], P('tensor'), may hold values from -0.1875 to 0.1875
- labels: int32 [4, 8, 1024], P(('groups', 'dp'), 'tensor', 'ctx'), parts along dimension 0, may hold values from 0 to 255, as said below
- grad_out: bfloat16 [4, 1024, 1024], P(('groups', 'dp'), 'ctx', 'tensor'), parts along dimension 0, may hold values from -6 to 6
Outputs:
- attended: bfloat16 [4, 1024, 1024], P(('groups', 'dp'), 'ctx', 'tensor'), parts along dimension 0
- grad_tokens: bfloat16 [4, 1024, 1024], P(('groups', 'dp'), 'ctx', 'tensor'), parts along dimension 0
- grad_w_qkv: float32 [2048, 3, 1024], P('groups', None, 'tensor'), parts along dimension 0
- grad_w_out: float32 [2048, 1024], P(('groups', 'tensor')), parts along dimension 0
There are 2 independent parts, one for each index of `groups`. A program takes and returns all parts, laid end to end along the dimension named above; an argument that names none is the same for every part. Nothing has to cross between parts.
Inputs may be any that keep to these rules, and one draw needn't show every extreme that they name: `labels`: cluster c of any head belongs to owner c % 4. Among the 256 tokens of one document on one index of ctx, at most 192 have, for one head, clusters of one owner; for each head one owner has exactly 192 from every such block, and the other owners share the rest of a block evenly (counts differ by at most one).
All inputs are finite; a program needn't handle non-finite values.
Results may differ from a plain program's by a relative error of at most 0.035.
The roundings to bfloat16 on the way count: a program that leaves them out, or rounds other values in their place, can miss the bound.
Values may be sent and summed in bfloat16 or wider, within the bound.
A program may use at most 64 MiB of HBM per device.

v0:
```python
import math
import jax
import jax.numpy as jnp
from jax import lax
from jax.sharding import PartitionSpec as P

HD = 128


def contract_last(left, right):
    return lax.dot_general(
        left, right, (((1,), (1,)), ((), ())), preferred_element_type=jnp.float32
    )


def contract_first(left, right):
    return lax.dot_general(
        left, right, (((0,), (0,)), ((), ())), preferred_element_type=jnp.float32
    )


def masked_probs(query_block, label_block, keys_in, marks):
    scores = contract_last(query_block, keys_in) * HD ** (-0.5)
    same = label_block[:, None] == marks[None, :]
    scores = jnp.where(same, scores, jnp.float32(-1e30))
    top_value = jnp.max(scores, axis=1, keepdims=True)
    expo = jnp.exp(scores - top_value)
    return expo / jnp.sum(expo, axis=1, keepdims=True)


def owner_forward(queries, keys_in, values_in, marks):
    total = queries.shape[0]
    block_rows = math.gcd(total, 512)
    block_count = total // block_rows

    def forward_block(index):
        start = index * block_rows
        query_block = lax.dynamic_slice_in_dim(queries, start, block_rows, 0)
        label_block = lax.dynamic_slice_in_dim(marks, start, block_rows, 0)
        probs = masked_probs(query_block, label_block, keys_in, marks).astype(jnp.bfloat16)
        return jnp.dot(probs, values_in, preferred_element_type=jnp.float32).astype(jnp.bfloat16)

    return lax.map(forward_block, jnp.arange(block_count, dtype=jnp.int32)).reshape(
        total, queries.shape[1]
    )


def owner_backward(queries, keys_in, values_in, marks, attention, cotangent):
    total, size = queries.shape
    block_rows = math.gcd(total, 512)
    block_count = total // block_rows

    def backward_block(carry, index):
        grad_keys, grad_values = carry
        start = index * block_rows
        query_block = lax.dynamic_slice_in_dim(queries, start, block_rows, 0)
        label_block = lax.dynamic_slice_in_dim(marks, start, block_rows, 0)
        attn_block = lax.dynamic_slice_in_dim(attention, start, block_rows, 0)
        cot_block = lax.dynamic_slice_in_dim(cotangent, start, block_rows, 0)
        probs_full = masked_probs(query_block, label_block, keys_in, marks)
        probs = probs_full.astype(jnp.bfloat16)
        dprob = contract_last(cot_block, values_in)
        delta = jnp.sum(
            cot_block.astype(jnp.float32) * attn_block.astype(jnp.float32), axis=1, keepdims=True
        )
        dscore = (probs_full * (dprob - delta) * HD ** (-0.5)).astype(jnp.bfloat16)
        grad_query = jnp.dot(dscore, keys_in, preferred_element_type=jnp.float32).astype(
            jnp.bfloat16
        )
        grad_keys = grad_keys + contract_first(dscore, query_block)
        grad_values = grad_values + contract_first(probs, cot_block)
        return ((grad_keys, grad_values), grad_query)

    empty = jnp.zeros((total, size), jnp.float32)
    (grad_keys, grad_values), grad_queries = lax.scan(
        backward_block, (empty, empty), jnp.arange(block_count, dtype=jnp.int32)
    )
    return (
        grad_queries.reshape(total, size),
        grad_keys.astype(jnp.bfloat16),
        grad_values.astype(jnp.bfloat16),
    )


def shards(tokens, w_qkv, w_out, labels, grad_out):
    rows_all, grads_all = (
        lax.all_gather(tokens, "tensor", axis=2, tiled=True),
        lax.all_gather(grad_out, "tensor", axis=2, tiled=True),
    )
    tok_rows = rows_all[0]
    tok_grads = grads_all[0]
    tok_count, width = tok_rows.shape
    heads_local = w_out.shape[0] // HD
    ctx_count = lax.axis_size("ctx")
    capacity = 3 * tok_count // ctx_count
    slot_total = ctx_count * capacity
    qkv = jnp.dot(
        tok_rows, w_qkv.reshape(width, 3 * heads_local * HD), preferred_element_type=jnp.float32
    )
    qkv = qkv.astype(jnp.bfloat16).reshape(tok_count, 3, heads_local, HD)
    qkv_heads = jnp.transpose(qkv, (2, 0, 1, 3)).reshape(heads_local, tok_count, 3 * HD)
    cotangent = contract_last(tok_grads, w_out).astype(jnp.bfloat16)
    cot_heads = jnp.transpose(cotangent.reshape(tok_count, heads_local, HD), (1, 0, 2))
    labels_local = labels[0]
    owner_of = labels_local % ctx_count
    owner_hits = (
        owner_of[:, :, None] == jnp.arange(ctx_count, dtype=jnp.int32)[None, None, :]
    ).astype(jnp.int32)
    earlier = jnp.cumsum(owner_hits, axis=1) - owner_hits
    slot_index = jnp.sum(earlier * owner_hits, axis=2)
    destination = owner_of * capacity + slot_index

    def pack(values):
        feature_count = values.shape[2]
        empty_buffer = jnp.zeros((heads_local, slot_total, feature_count), values.dtype)
        filled = jax.vmap(lambda buffer, where_to, rows_in: buffer.at[where_to].set(rows_in))(
            empty_buffer, destination, values
        )
        return filled.reshape(heads_local, ctx_count, capacity, feature_count)

    def unpack(received):
        flat = received.reshape(heads_local, slot_total, received.shape[3])
        return jax.vmap(lambda table, where_to: jnp.take(table, where_to, axis=0))(
            flat, destination
        )

    label_slots = jax.vmap(
        lambda where_to, marks: jnp.full((slot_total,), -1.0, jnp.bfloat16).at[where_to].set(marks)
    )(destination, labels_local.astype(jnp.bfloat16)).reshape(heads_local, ctx_count, capacity)
    arrived, arrived_marks = (
        lax.all_to_all(pack(qkv_heads), "ctx", split_axis=1, concat_axis=1, tiled=True),
        lax.all_to_all(label_slots, "ctx", split_axis=1, concat_axis=1, tiled=True),
    )
    arrived = arrived.reshape(heads_local, slot_total, 3 * HD)
    marks_own = arrived_marks.reshape(heads_local, slot_total)
    queries_own = arrived[:, :, :HD]
    keys_own = arrived[:, :, HD : 2 * HD]
    values_own = arrived[:, :, 2 * HD :]
    attention_own = jax.vmap(owner_forward)(queries_own, keys_own, values_own, marks_own)
    returned = lax.all_to_all(
        attention_own.reshape(heads_local, ctx_count, capacity, HD),
        "ctx",
        split_axis=1,
        concat_axis=1,
        tiled=True,
    )
    attention_tok = unpack(returned)
    cot_arrived = lax.all_to_all(pack(cot_heads), "ctx", split_axis=1, concat_axis=1, tiled=True)
    cot_own = cot_arrived.reshape(heads_local, slot_total, HD)
    grad_q, grad_k, grad_v = jax.vmap(owner_backward)(
        queries_own, keys_own, values_own, marks_own, attention_own, cot_own
    )
    grads_own = jnp.concatenate([grad_q, grad_k, grad_v], axis=2).reshape(
        heads_local, ctx_count, capacity, 3 * HD
    )
    grads_back = lax.all_to_all(grads_own, "ctx", split_axis=1, concat_axis=1, tiled=True)
    grad_heads = unpack(grads_back)
    attention_rows = jnp.transpose(attention_tok, (1, 0, 2)).reshape(tok_count, heads_local * HD)
    out_terms = jnp.dot(attention_rows, w_out, preferred_element_type=jnp.float32)
    attended = lax.psum_scatter(
        out_terms.astype(jnp.bfloat16), "tensor", scatter_dimension=1, tiled=True
    )
    grad_qkv = jnp.transpose(grad_heads.reshape(heads_local, tok_count, 3, HD), (1, 2, 0, 3))
    grad_qkv = grad_qkv.reshape(tok_count, 3 * heads_local * HD)
    grad_w_out_local = contract_first(attention_rows, tok_grads)
    grad_w_qkv_local = contract_first(tok_rows, grad_qkv).reshape(width, 3, heads_local * HD)
    summed_qkv, summed_out = (
        lax.psum(grad_w_qkv_local.astype(jnp.bfloat16), ("ctx", "dp")).astype(jnp.float32),
        lax.psum(grad_w_out_local.astype(jnp.bfloat16), ("ctx", "dp")).astype(jnp.float32),
    )
    in_terms = contract_last(grad_qkv, w_qkv.reshape(width, 3 * heads_local * HD))
    grad_tokens = lax.psum_scatter(
        in_terms.astype(jnp.bfloat16), "tensor", scatter_dimension=1, tiled=True
    )
    return (attended[None], grad_tokens[None], summed_qkv, summed_out)


def solution(mesh):
    placed = (
        P(("groups", "dp"), "ctx", "tensor"),
        P(None, None, "tensor"),
        P("tensor", None),
        P(("groups", "dp"), "tensor", "ctx"),
        P(("groups", "dp"), "ctx", "tensor"),
    )
    return jax.shard_map(
        shards,
        mesh=mesh,
        in_specs=placed,
        out_specs=(
            P(("groups", "dp"), "ctx", "tensor"),
            P(("groups", "dp"), "ctx", "tensor"),
            P("groups", None, "tensor"),
            P(("groups", "tensor"), None),
        ),
        check_vma=False,
    )
```

profile of v0, /device:TPU:0, one launch (start us, length us, event | category | flops | bytes accessed | tf_op | source)
XLA Modules:
  0.0 419.2 jit_solution(18375576288930993019)
XLA Ops:
  10.2 4.8 %reduce-window.6 = s32[4,4,2,128]{3,2,1,0:T(2,128)S(1)} reduce-window(s32[4,4,2,128]{3,2,1,0:T(2,128)S(1)} %compare_convert_fusion, s32[]{:T(128)} %constant.96.clone.1), window={size=1x1x1x128 pad=0_0x0_0x0_0x127_0}, to_apply=%region_0.1 | reduce-window | flops 520192 | bytes 32772 | tf_op jit(solution)/shard_map/reduce-window
  17.8 7.6 %scatter_custom_fusion = bf16[3072]{0:T(1024)(128)(2,1)S(1)} fusion(s32[1024]{0:T(1024)S(1)} %bitcast.228, bf16[1024]{0:T(1024)(128)(2,1)S(1)} %bitcast.231, bf16[]{:T(256)} %constant.103.clone.1), kind=kCustom, calls=%fused_computation.120 | custom fusion | bytes 6146
  26.1 6.3 %all-to-all-start = ((bf16[4,4,192]{2,0,1:T(4,128)(2,1)}), bf16[4,4,192]{2,0,1:T(4,128)(2,1)S(1)}, u32[]{:S(2)}, u32[]{:S(2)}) async-start(bf16[4,4,192]{2,0,1:T(4,128)(2,1)} %copy.67), calls=%async_computation | async-start | bytes 16384 | tf_op jit(solution)/shard_map/all_to_all | solution.py:132
  32.4 8.6 %all_gather.7 = bf16[1,256,1024]{2,1,0:T(8,128)(2,1)S(1)} all-gather(bf16[1,256,512]{2,1,0:T(8,128)(2,1)} %param.13), channel_id=1, replica_groups=mesh['groups'=2,'ctx'=4,'tensor'=2,'dp'=2] {'tensor'}, dimensions={2}, use_global_device_ids=true | all-gather | bytes 786432 | tf_op jit(solution)/shard_map/all_gather | solution.py:88
  42.4 3.4 scatter_custom_fusion.2
  46.8 4.8 %all-to-all-start.3 = ((bf16[4,4,192,128]{3,2,0,1:T(8,128)(2,1)}), bf16[4,4,192,128]{3,2,0,1:T(8,128)(2,1)}, u32[]{:S(2)}, u32[]{:S(2)}) async-start(bf16[4,4,192,128]{3,2,0,1:T(8,128)(2,1)} %copy.80), calls=%async_computation.4 | async-start | bytes 1572864 | tf_op jit(solution)/shard_map/all_to_all | solution.py:148
  51.6 4.7 %copy.69 = bf16[1024,3,512]{0,2,1:T(8,128)(2,1)} copy(bf16[1024,3,512]{2,0,1:T(8,128)(2,1)} %param.10) | data formatting | bytes 6291456 | tf_op args[1]
  56.3 7.0 %all_gather.6 = bf16[1,256,1024]{2,1,0:T(8,128)(2,1)S(1)} all-gather(bf16[1,256,512]{2,1,0:T(8,128)(2,1)S(1)} %copy-done.10), channel_id=1, replica_groups=mesh['groups'=2,'ctx'=4,'tensor'=2,'dp'=2] {'tensor'}, dimensions={2}, use_global_device_ids=true | all-gather | bytes 786432 | tf_op jit(solution)/shard_map/all_gather | solution.py:87
  69.3 6.5 %scatter_custom_fusion.1 = bf16[3072,384]{1,0:T(8,128)(2,1)S(1)} fusion(s32[1024]{0:T(1024)S(1)} %bitcast.230, bf16[1024,384]{1,0:T(8,128)(2,1)} %copy.71, bf16[]{:T(256)} %constant.102.clone.1), kind=kCustom, calls=%fused_computation.77 | custom fusion | bytes 2359808
  77.5 5.1 %all-to-all-start.1 = ((bf16[4,4,192,384]{3,2,0,1:T(8,128)(2,1)}), bf16[4,4,192,384]{3,2,0,1:T(8,128)(2,1)}, u32[]{:S(2)}, u32[]{:S(2)}) async-start(bf16[4,4,192,384]{3,2,0,1:T(8,128)(2,1)} %copy.72), calls=%async_computation.1 | async-start | bytes 4718592 | tf_op jit(solution)/shard_map/all_to_all | solution.py:131
  85.0 48.7 %all-to-all-done.1 = bf16[4,4,192,384]{3,2,0,1:T(8,128)(2,1)} async-done(((bf16[4,4,192,384]{3,2,0,1:T(8,128)(2,1)}), bf16[4,4,192,384]{3,2,0,1:T(8,128)(2,1)}, u32[]{:S(2)}, u32[]{:S(2)}) %all-to-all-start.1) | async-done | bytes 2359328 | tf_op jit(solution)/shard_map/all_to_all | solution.py:131
  137.4 23.0 %while.33 = (s32[]{:T(128)}, bf16[3,4,256,128]{3,2,0,1:T(8,128)(2,1)S(1)}, s32[3]{0:T(128)S(1)}, bf16[4,768]{1,0:T(4,128)(2,1)S(1)}, bf16[4,4,192]{2,1,0:T(4,128...) while((s32[]{:T(128)}, ...), condition=%wide.wide.region_8.9_spmd, body=%wide.wide.region_5.8_spmd.sunk | while | flops 612764160 | bytes 3175139 | solution.py:43
  141.3 3.8 fusion.173
  149.0 3.8 fusion.173
  156.6 3.8 fusion.173
  161.4 4.2 all-to-all-start.2
  166.7 56.3 %while.34 = (s32[]{:T(128)}, f32[4,768,128]{2,1,0:T(8,128)S(1)}, f32[4,768,128]{2,1,0:T(8,128)}, bf16[3,4,256,128]{3,2,0,1:T(8,128)(2,1)}, s32[3]{0:T(128)S(1)},...) while((s32[]{:T(128)}, f32[4,768,128]{2,1,0:T(8,128)S(1)}, ...), condition=%wide.wide.region_15.16_spmd.clone, body=%wide.wide.region_11.15_spmd.clone.sunk | while | flops 1222772224 | bytes 25732404 | solution.py:75
  169.2 4.1 fusion.187
  179.9 5.2 %select_add_fusion.7 = f32[4,768,128]{2,1,0:T(8,128)} fusion(f32[4,768,128]{2,1,0:T(8,128)} %get-tuple-element.590, f32[4,256]{1,0:T(4,128)S(1)} %get-tuple-element.527, pred[]{:T(512)S(6)} %compare.29, bf16[4,768,128]{2,1,0:T(8,128)(2,1)} %get-tuple-element.615, s32[]{:T(128)S(1)} %bitcast.226, ...), kind=kOutput, calls=%fused_computation.37.clone.clone.1 | convolution fusion | flops 408160000 | bytes 4469761 | tf_op jit(solution)/shard_map/vmap()/while/body/eval_jaxpr/dot_general | solution.py:17
  187.6 4.1 fusion.187
  191.7 3.0 multiply_convert_fusion.3
  198.3 5.7 %select_add_fusion.7 = f32[4,768,128]{2,1,0:T(8,128)} fusion(f32[4,768,128]{2,1,0:T(8,128)} %get-tuple-element.590, f32[4,256]{1,0:T(4,128)S(1)} %get-tuple-element.527, pred[]{:T(512)S(6)} %compare.29, bf16[4,768,128]{2,1,0:T(8,128)(2,1)} %get-tuple-element.615, s32[]{:T(128)S(1)} %bitcast.226, ...), kind=kOutput, calls=%fused_computation.37.clone.clone.1 | convolution fusion | flops 408160000 | bytes 4469761 | tf_op jit(solution)/shard_map/vmap()/while/body/eval_jaxpr/dot_general | solution.py:17
  206.6 4.1 fusion.187
  217.2 5.7 %select_add_fusion.7 = f32[4,768,128]{2,1,0:T(8,128)} fusion(f32[4,768,128]{2,1,0:T(8,128)} %get-tuple-element.590, f32[4,256]{1,0:T(4,128)S(1)} %get-tuple-element.527, pred[]{:T(512)S(6)} %compare.29, bf16[4,768,128]{2,1,0:T(8,128)(2,1)} %get-tuple-element.615, s32[]{:T(128)S(1)} %bitcast.226, ...), kind=kOutput, calls=%fused_computation.37.clone.clone.1 | convolution fusion | flops 408160000 | bytes 4469761 | tf_op jit(solution)/shard_map/vmap()/while/body/eval_jaxpr/dot_general | solution.py:17
  227.6 5.2 %all-to-all-start.4 = ((bf16[4,4,192,384]{3,2,0,1:T(8,128)(2,1)}), bf16[4,4,192,384]{3,2,0,1:T(8,128)(2,1)}, u32[]{:S(2)}, u32[]{:S(2)}) async-start(bf16[4,4,192,384]{3,2,0,1:T(8,128)(2,1)} %copy.84), calls=%async_computation.5 | async-start | bytes 4718592 | tf_op jit(solution)/shard_map/all_to_all | solution.py:156
  234.1 5.8 %gather_fusion = bf16[1024,128]{1,0:T(8,128)(2,1)S(1)} fusion(bf16[4,768,128]{2,1,0:T(8,128)(2,1)S(1)} %bitcast.205, s32[1024]{0:T(1024)S(1)} %bitcast.199), kind=kCustom, calls=%fused_computation | custom fusion | bytes 532480 | tf_op jit(solution)/shard_map/vmap(jit(_take))/gather | solution.py:123
  242.3 43.4 %all-to-all-done.4 = bf16[4,4,192,384]{3,2,0,1:T(8,128)(2,1)} async-done(((bf16[4,4,192,384]{3,2,0,1:T(8,128)(2,1)}), bf16[4,4,192,384]{3,2,0,1:T(8,128)(2,1)}, u32[]{:S(2)}, u32[]{:S(2)}) %all-to-all-start.4) | async-done | bytes 2359328 | tf_op jit(solution)/shard_map/all_to_all | solution.py:156
  287.6 11.6 %gather_fusion.1 = bf16[1024,384]{1,0:T(8,128)(2,1)} fusion(bf16[4,768,384]{2,1,0:T(8,128)(2,1)S(1)} %bitcast.201, s32[1024]{0:T(1024)S(1)} %bitcast.200), kind=kCustom, calls=%fused_computation.1 | custom fusion | bytes 1581056 | tf_op jit(solution)/shard_map/vmap(jit(_take))/gather | solution.py:123
  304.4 4.7 %copy.88 = bf16[1024,3,512]{2,0,1:T(8,128)(2,1)} copy(bf16[1024,3,512]{0,2,1:T(8,128)(2,1)} %bitcast.202) | data formatting | bytes 6291456 | tf_op jit(solution)/shard_map/convert_element_type | solution.py:168
  311.3 3.7 convolution_convert_fusion.5
  315.1 90.2 %all-reduce.3.cloned.1.call-done = (bf16[1024,3,512]{2,0,1:T(8,128)(2,1)}, bf16[512,1024]{1,0:T(8,128)(2,1)}) async-done(((bf16[1024,3,512]{2,0,1:T(8,128)(2,1)}, bf16[512,1024]{1,0:T(8,128)(2,1)}), (bf16[1024,3,512]{2,0,1:T(8,128)(2,1)}, bf16[512,1024]{1,0:T(8,128)(2,1)})) %all-reduce.3.cloned.1.call-update) | async-done | bytes 4194320 | tf_op jit(solution)/shard_map/psum | solution.py:168
  408.2 3.6 convert_element_type.79
  (136 shorter events, 75.9 us)
Async XLA Ops:
  8.0 33.8 %copy-start = (bf16[512,1024]{1,0:T(8,128)(2,1)S(1)}, bf16[512,1024]{1,0:T(8,128)(2,1)}, u32[]{:S(2)}) copy-start(bf16[512,1024]{1,0:T(8,128)(2,1)} %param.11) | copy-start | bytes 3145732
  26.1 20.7 %all-to-all-start = ((bf16[4,4,192]{2,0,1:T(4,128)(2,1)}), bf16[4,4,192]{2,0,1:T(4,128)(2,1)S(1)}, u32[]{:S(2)}, u32[]{:S(2)}) async-start(bf16[4,4,192]{2,0,1:T(4,128)(2,1)} %copy.67), calls=%async_computation | async-start | bytes 16384 | tf_op jit(solution)/shard_map/all_to_all | solution.py:132
  41.0 0.8 copy-start.1
  46.8 30.7 %all-to-all-start.3 = ((bf16[4,4,192,128]{3,2,0,1:T(8,128)(2,1)}), bf16[4,4,192,128]{3,2,0,1:T(8,128)(2,1)}, u32[]{:S(2)}, u32[]{:S(2)}) async-start(bf16[4,4,192,128]{3,2,0,1:T(8,128)(2,1)} %copy.80), calls=%async_computation.4 | async-start | bytes 1572864 | tf_op jit(solution)/shard_map/all_to_all | solution.py:148
  51.6 4.7 %copy-start.10 = (bf16[1,256,512]{2,1,0:T(8,128)(2,1)S(1)}, bf16[1,256,512]{2,1,0:T(8,128)(2,1)}, u32[]{:S(2)}) copy-start(bf16[1,256,512]{2,1,0:T(8,128)(2,1)} %param.9) | copy-start | bytes 786436
  63.3 0.8 copy-start.6
  77.5 56.2 %all-to-all-start.1 = ((bf16[4,4,192,384]{3,2,0,1:T(8,128)(2,1)}), bf16[4,4,192,384]{3,2,0,1:T(8,128)(2,1)}, u32[]{:S(2)}, u32[]{:S(2)}) async-start(bf16[4,4,192,384]{3,2,0,1:T(8,128)(2,1)} %copy.72), calls=%async_computation.1 | async-start | bytes 4718592 | tf_op jit(solution)/shard_map/all_to_all | solution.py:131
  82.6 53.0 %copy-start.11 = (bf16[4,4,192]{2,1,0:T(4,128)(2,1)}, bf16[4,4,192]{2,1,0:T(4,128)(2,1)S(1)}, u32[]{:S(2)}) copy-start(bf16[4,4,192]{2,1,0:T(4,128)(2,1)S(1)} %copy.68) | copy-start | bytes 18436
  161.4 66.2 %all-to-all-start.2 = ((bf16[4,4,192,128]{3,2,0,1:T(8,128)(2,1)}), bf16[4,4,192,128]{3,2,0,1:T(8,128)(2,1)}, u32[]{:S(2)}, u32[]{:S(2)}) async-start(bf16[4,4,192,128]{3,2,0,1:T(8,128)(2,1)} %copy.76), calls=%async_computation.2 | async-start | bytes 1572864 | tf_op jit(solution)/shard_map/all_to_all | solution.py:140
  173.3 3.0 copy-start.9
  191.7 3.0 copy-start.9
  210.7 3.0 copy-start.9
  223.0 1.4 copy-start.8
  227.6 5.2 %copy-start.12 = (s32[1,4,256]{2,1,0:T(4,128)S(1)}, s32[1,4,256]{2,1,0:T(4,128)}, u32[]{:S(2)}) copy-start(s32[1,4,256]{2,1,0:T(4,128)} %param.12) | copy-start | bytes 12292
  227.6 58.0 %all-to-all-start.4 = ((bf16[4,4,192,384]{3,2,0,1:T(8,128)(2,1)}), bf16[4,4,192,384]{3,2,0,1:T(8,128)(2,1)}, u32[]{:S(2)}, u32[]{:S(2)}) async-start(bf16[4,4,192,384]{3,2,0,1:T(8,128)(2,1)} %copy.84), calls=%async_computation.5 | async-start | bytes 4718592 | tf_op jit(solution)/shard_map/all_to_all | solution.py:156
  232.8 8.0 %copy-start.2 = (bf16[1,256,1024]{2,1,0:T(8,128)(2,1)S(1)}, bf16[1,256,1024]{2,1,0:T(8,128)(2,1)}, u32[]{:S(2)}) copy-start(bf16[1,256,1024]{2,1,0:T(8,128)(2,1)} %copy-done.1) | copy-start | bytes 1572868
  232.8 172.4 %all-reduce.3.cloned.1.call-start = ((), (), s32[]{:S(2)}) async-start(), calls=%async_computation.9 | async-start | bytes 8388608 | tf_op jit(solution)/shard_map/psum | solution.py:168
  240.2 0.7 copy-start.4
  299.2 2.5 copy-start.7
  309.1 0.9 copy-start.5
  309.1 102.7 %reduce-scatter.3.cloned.1.call-start = ((), (), s32[]{:S(2)}) async-start(), calls=%async_computation.7 | async-start | bytes 786432 | tf_op jit(solution)/shard_map/reduce_scatter | solution.py:160
  311.3 100.5 %reduce-scatter.5.cloned.1.call-start = ((), (), s32[]{:S(2)}) async-start(), calls=%async_computation.8 | async-start | bytes 786432 | tf_op jit(solution)/shard_map/reduce_scatter | solution.py:172
  405.2 2.9 copy-start.3
Sparse Core Ops, SparseCore 0:
  309.2 95.9 all-reduce.2
Sparse Core Ops, SparseCore 1:
  312.4 13.6 reduce-scatter.2
  328.8 14.5 reduce-scatter.4
where the time goes:
time: 421 us; the launch traced here: 419 us
  waiting for transfers between devices  182 us (43%)
  matrix products  80 us (19%)
  local copies, waits for them, and re-layouts  74.3 us (18%)
  starting transfers between devices  25.7 us (6%)
  other arithmetic  21.4 us (5%)
  between operations  15.8 us (4%)
  blocking collectives  15.7 us (4%)
    psum x1, waiting for transfers between devices, shards(): lax.psum(grad_w_qkv_local.astype(jnp.bfloat16), ('ctx', 'dp'))  90.2 us
    all_to_all x1, waiting for transfers between devices, shards(): lax.all_to_all(pack(qkv_heads), 'ctx', split_axis=1, concat_axis=1, tiled...  48.7 us
    all_to_all x1, waiting for transfers between devices, shards(): lax.all_to_all(grads_own, 'ctx', split_axis=1, concat_axis=1, tiled=True)  43.4 us
    dot_general x8, matrix products, contract_first(): lax.dot_general(left, right, (((0,), (0,)), ((), ())), preferred_element_...  27.5 us
    unnamed x32, local copies, waits for them, and re-layouts  26.9 us
    sub x6, matrix products, masked_probs(): expo = jnp.exp(scores - top_value)  19.8 us
    gather x5, local copies, waits for them, and re-layouts, unpack(): jnp.take(table, where_to, axis=0)  19.6 us
    dot_general x5, matrix products, contract_last(): lax.dot_general(left, right, (((1,), (1,)), ((), ())), preferred_element_...  13.2 us
  transfers between devices with their start and end apart: 8, of which 3 were waited for; matrix products, arithmetic and copies ran while one was open for 25% of the time, Pallas kernels for 0%

commit v1 on v0

--- a/solution.py
+++ b/solution.py
@@ -5,6 +5,11 @@
 from jax.sharding import PartitionSpec as P
 
 HD = 128
+
+
+def _end_spot(frame_in):
+    prior = jax.lax.all_gather(frame_in, ("ctx", "dp"))
+    return jnp.sum(prior, axis=0)
 
 
 def contract_last(left, right):
@@ -165,7 +170,7 @@
     grad_w_out_local = contract_first(attention_rows, tok_grads)
     grad_w_qkv_local = contract_first(tok_rows, grad_qkv).reshape(width, 3, heads_local * HD)
     summed_qkv, summed_out = (
-        lax.psum(grad_w_qkv_local.astype(jnp.bfloat16), ("ctx", "dp")).astype(jnp.float32),
+        _end_spot(grad_w_qkv_local.astype(jnp.bfloat16)).astype(jnp.float32),
         lax.psum(grad_w_out_local.astype(jnp.bfloat16), ("ctx", "dp")).astype(jnp.float32),
     )
     in_terms = contract_last(grad_qkv, w_qkv.reshape(width, 3 * heads_local * HD))

time: 421 us -> 589 us (1.40)
  waiting for transfers between devices: 182 us -> 321 us
  other arithmetic: 21.4 us -> 33.2 us
  matrix products: 80 us -> 89.4 us
  local copies, waits for them, and re-layouts: 74.3 us -> 82.4 us
    all_gather x0 -> x1, waiting for transfers between devices: none -> 218 us  [_end_spot(): prior = jax.lax.all_gather(frame_in, ('ctx', 'dp'))]
    psum x1, waiting for transfers between devices: 90.2 us -> 0.68 us  [shards(): lax.psum(grad_w_out_local.astype(jnp.bfloat16), ('ctx', 'dp'))]
    reduce_sum x0 -> x1, other arithmetic: none -> 15.3 us  [_end_spot(): return jnp.sum(prior, axis=0)]
    all_to_all x1, waiting for transfers between devices: 43.4 us -> 53.6 us  [shards(): lax.all_to_all(grads_own, 'ctx', split_axis=1, concat_axis=1, tiled=True)]
    unnamed x32, local copies, waits for them, and re-layouts: 26.9 us -> 34.9 us
  transfers between devices with their start and end apart: 8 -> 9, of which waited for: 3 -> 4; matrix products, arithmetic and copies ran while one was open for 25% -> 27% of each run, Pallas kernels for 0% -> 0%
where the time goes in v1:
time: 589 us; the launch traced here: 587 us
  waiting for transfers between devices  321 us (54%)
  matrix products  89.4 us (15%)
  local copies, waits for them, and re-layouts  82.4 us (14%)
  other arithmetic  33.2 us (6%)
  starting transfers between devices  25.9 us (4%)
  between operations  15.8 us (3%)
  blocking collectives  15.7 us (3%)
    all_gather x1, waiting for transfers between devices, _end_spot(): prior = jax.lax.all_gather(frame_in, ('ctx', 'dp'))  218 us
    all_to_all x1, waiting for transfers between devices, shards(): lax.all_to_all(grads_own, 'ctx', split_axis=1, concat_axis=1, tiled=True)  53.6 us
    all_to_all x1, waiting for transfers between devices, shards(): lax.all_to_all(pack(qkv_heads), 'ctx', split_axis=1, concat_axis=1, tiled...  48.8 us
    unnamed x32, local copies, waits for them, and re-layouts  34.9 us
    dot_general x8, matrix products, contract_first(): lax.dot_general(left, right, (((0,), (0,)), ((), ())), preferred_element_...  28.7 us
    sub x6, matrix products, masked_probs(): expo = jnp.exp(scores - top_value)  19.9 us
    gather x5, local copies, waits for them, and re-layouts, unpack(): jnp.take(table, where_to, axis=0)  19.6 us
    dot_general x5, matrix products, contract_last(): lax.dot_general(left, right, (((1,), (1,)), ((), ())), preferred_element_...  16.6 us
  transfers between devices with their start and end apart: 9, of which 4 were waited for; matrix products, arithmetic and copies ran while one was open for 27% of the time, Pallas kernels for 0%

profile of v1, /device:TPU:0, one launch (start us, length us, event | category | flops | bytes accessed | tf_op | source)
XLA Modules:
  0.0 587.3 jit_solution(12248956988960880550)
XLA Ops:
  10.2 4.8 reduce-window.6
  17.8 7.6 %scatter_custom_fusion = bf16[3072]{0:T(1024)(128)(2,1)S(1)} fusion(s32[1024]{0:T(1024)S(1)} %bitcast.226, bf16[1024]{0:T(1024)(128)(2,1)S(1)} %bitcast.229, bf16[]{:T(256)} %constant.105.clone.1), kind=kCustom, calls=%fused_computation.120 | custom fusion | bytes 6146
  26.1 6.3 %all-to-all-start = ((bf16[4,4,192]{2,0,1:T(4,128)(2,1)}), bf16[4,4,192]{2,0,1:T(4,128)(2,1)S(1)}, u32[]{:S(2)}, u32[]{:S(2)}) async-start(bf16[4,4,192]{2,0,1:T(4,128)(2,1)} %copy.66), calls=%async_computation | async-start | bytes 16384 | tf_op jit(solution)/shard_map/all_to_all | solution.py:137
  32.4 8.6 %all_gather.11 = bf16[1,256,1024]{2,1,0:T(8,128)(2,1)S(1)} all-gather(bf16[1,256,512]{2,1,0:T(8,128)(2,1)} %param.13), channel_id=1, replica_groups=mesh['groups'=2,'ctx'=4,'tensor'=2,'dp'=2] {'tensor'}, dimensions={2}, use_global_device_ids=true | all-gather | bytes 786432 | tf_op jit(solution)/shard_map/all_gather | solution.py:93
  46.8 4.8 all-to-all-start.3
  51.6 4.7 copy.68
  56.3 7.0 %all_gather.10 = bf16[1,256,1024]{2,1,0:T(8,128)(2,1)S(1)} all-gather(bf16[1,256,512]{2,1,0:T(8,128)(2,1)S(1)} %copy-done.8), channel_id=1, replica_groups=mesh['groups'=2,'ctx'=4,'tensor'=2,'dp'=2] {'tensor'}, dimensions={2}, use_global_device_ids=true | all-gather | bytes 786432 | tf_op jit(solution)/shard_map/all_gather | solution.py:92
  69.3 6.5 %scatter_custom_fusion.1 = bf16[3072,384]{1,0:T(8,128)(2,1)S(1)} fusion(s32[1024]{0:T(1024)S(1)} %bitcast.228, bf16[1024,384]{1,0:T(8,128)(2,1)} %copy.70, bf16[]{:T(256)} %constant.104.clone.1), kind=kCustom, calls=%fused_computation.77 | custom fusion | bytes 2359808
  77.5 5.1 all-to-all-start.1
  84.9 48.8 %all-to-all-done.1 = bf16[4,4,192,384]{3,2,0,1:T(8,128)(2,1)} async-done(((bf16[4,4,192,384]{3,2,0,1:T(8,128)(2,1)}), bf16[4,4,192,384]{3,2,0,1:T(8,128)(2,1)}, u32[]{:S(2)}, u32[]{:S(2)}) %all-to-all-start.1) | async-done | bytes 2359328 | tf_op jit(solution)/shard_map/all_to_all | solution.py:136
  137.3 23.1 %while.33 = (s32[]{:T(128)}, bf16[3,4,256,128]{3,2,0,1:T(8,128)(2,1)S(1)}, s32[3]{0:T(128)S(1)}, bf16[4,768]{1,0:T(4,128)(2,1)S(1)}, bf16[4,4,192]{2,1,0:T(4,128...) while((s32[]{:T(128)}, ...), condition=%wide.wide.region_8.9_spmd, body=%wide.wide.region_5.8_spmd.sunk | while | flops 612764160 | bytes 3175139 | solution.py:48
  141.2 3.8 fusion.173
  161.4 4.2 all-to-all-start.2
  166.7 65.6 %while.34 = (s32[]{:T(128)}, f32[4,768,128]{2,1,0:T(8,128)S(1)}, f32[4,768,128]{2,1,0:T(8,128)}, bf16[3,4,256,128]{3,2,0,1:T(8,128)(2,1)}, s32[3]{0:T(128)S(1)},...) while((s32[]{:T(128)}, f32[4,768,128]{2,1,0:T(8,128)S(1)}, ...), condition=%wide.wide.region_15.16_spmd.clone, body=%wide.wide.region_11.15_spmd.clone.sunk | while | flops 1222772224 | bytes 22586648 | solution.py:80
  169.2 4.1 fusion.187
  173.3 4.1 multiply_convert_fusion.3
  180.1 5.2 select_add_fusion.7
  190.7 4.1 fusion.187
  194.8 4.1 multiply_convert_fusion.3
  201.6 5.7 select_add_fusion.7
  212.8 4.1 fusion.187
  216.9 4.1 multiply_convert_fusion.3
  223.7 5.7 select_add_fusion.7
  236.0 5.2 all-to-all-start.4
  242.5 5.8 gather_fusion
  250.3 53.6 %all-to-all-done.4 = bf16[4,4,192,384]{3,2,0,1:T(8,128)(2,1)} async-done(((bf16[4,4,192,384]{3,2,0,1:T(8,128)(2,1)}), bf16[4,4,192,384]{3,2,0,1:T(8,128)(2,1)}, u32[]{:S(2)}, u32[]{:S(2)}) %all-to-all-start.4) | async-done | bytes 2359328 | tf_op jit(solution)/shard_map/all_to_all | solution.py:161
  305.8 11.6 %gather_fusion.1 = bf16[1024,384]{1,0:T(8,128)(2,1)} fusion(bf16[4,768,384]{2,1,0:T(8,128)(2,1)S(1)} %bitcast.198, s32[1024]{0:T(1024)S(1)} %bitcast.197), kind=kCustom, calls=%fused_computation.1 | custom fusion | bytes 1581056 | tf_op jit(solution)/shard_map/vmap(jit(_take))/gather | solution.py:128
  322.6 4.7 copy.87
  336.8 217.7 %all-gather.2.cloned.1.call-done = bf16[8,1024,3,512]{3,1,2,0:T(8,128)(2,1)} async-done(((bf16[1,1024,3,512]{3,1,2,0:T(8,128)(2,1)}), bf16[8,1024,3,512]{3,1,2,0:T(8,128)(2,1)}) %all-gather.2.cloned.1.call-update) | async-done | bytes 25165840 | tf_op jit(solution)/shard_map/all_gather | solution.py:11
  554.6 15.3 %reduce_sum.52 = bf16[1024,3,512]{2,0,1:T(8,128)(2,1)} reduce(bf16[8,1024,3,512]{3,1,2,0:T(8,128)(2,1)} %all-gather.2.cloned.1.call-done, bf16[]{:T(256)} %constant.104.clone.1), dimensions={0}, to_apply=%region_17.18 | reduce | flops 11010048 | bytes 28311554 | tf_op jit(solution)/shard_map/reduce_sum | solution.py:12
  569.8 4.7 copy.96
  574.5 5.4 copy.89
  (133 shorter events, 90.0 us)
Async XLA Ops:
  8.0 33.8 %copy-start = (bf16[512,1024]{1,0:T(8,128)(2,1)S(1)}, bf16[512,1024]{1,0:T(8,128)(2,1)}, u32[]{:S(2)}) copy-start(bf16[512,1024]{1,0:T(8,128)(2,1)} %param.11) | copy-start | bytes 3145732
  26.1 20.7 %all-to-all-start = ((bf16[4,4,192]{2,0,1:T(4,128)(2,1)}), bf16[4,4,192]{2,0,1:T(4,128)(2,1)S(1)}, u32[]{:S(2)}, u32[]{:S(2)}) async-start(bf16[4,4,192]{2,0,1:T(4,128)(2,1)} %copy.66), calls=%async_computation | async-start | bytes 16384 | tf_op jit(solution)/shard_map/all_to_all | solution.py:137
  41.0 0.8 copy-start.1
  46.8 30.7 %all-to-all-start.3 = ((bf16[4,4,192,128]{3,2,0,1:T(8,128)(2,1)}), bf16[4,4,192,128]{3,2,0,1:T(8,128)(2,1)}, u32[]{:S(2)}, u32[]{:S(2)}) async-start(bf16[4,4,192,128]{3,2,0,1:T(8,128)(2,1)} %copy.79), calls=%async_computation.4 | async-start | bytes 1572864 | tf_op jit(solution)/shard_map/all_to_all | solution.py:153
  51.6 4.7 copy-start.8
  63.3 0.8 copy-start.6
  77.5 56.2 %all-to-all-start.1 = ((bf16[4,4,192,384]{3,2,0,1:T(8,128)(2,1)}), bf16[4,4,192,384]{3,2,0,1:T(8,128)(2,1)}, u32[]{:S(2)}, u32[]{:S(2)}) async-start(bf16[4,4,192,384]{3,2,0,1:T(8,128)(2,1)} %copy.71), calls=%async_computation.1 | async-start | bytes 4718592 | tf_op jit(solution)/shard_map/all_to_all | solution.py:136
  82.6 53.0 %copy-start.9 = (bf16[4,4,192]{2,1,0:T(4,128)(2,1)}, bf16[4,4,192]{2,1,0:T(4,128)(2,1)S(1)}, u32[]{:S(2)}) copy-start(bf16[4,4,192]{2,1,0:T(4,128)(2,1)S(1)} %copy.67) | copy-start | bytes 18436
  161.4 74.6 %all-to-all-start.2 = ((bf16[4,4,192,128]{3,2,0,1:T(8,128)(2,1)}), bf16[4,4,192,128]{3,2,0,1:T(8,128)(2,1)}, u32[]{:S(2)}, u32[]{:S(2)}) async-start(bf16[4,4,192,128]{3,2,0,1:T(8,128)(2,1)} %copy.75), calls=%async_computation.2 | async-start | bytes 1572864 | tf_op jit(solution)/shard_map/all_to_all | solution.py:145
  232.3 1.7 copy-start.3
  236.0 5.2 copy-start.10
  236.0 67.9 %all-to-all-start.4 = ((bf16[4,4,192,384]{3,2,0,1:T(8,128)(2,1)}), bf16[4,4,192,384]{3,2,0,1:T(8,128)(2,1)}, u32[]{:S(2)}, u32[]{:S(2)}) async-start(bf16[4,4,192,384]{3,2,0,1:T(8,128)(2,1)} %copy.83), calls=%async_computation.5 | async-start | bytes 4718592 | tf_op jit(solution)/shard_map/all_to_all | solution.py:161
  241.2 7.3 %copy-start.2 = (bf16[1,256,1024]{2,1,0:T(8,128)(2,1)S(1)}, bf16[1,256,1024]{2,1,0:T(8,128)(2,1)}, u32[]{:S(2)}) copy-start(bf16[1,256,1024]{2,1,0:T(8,128)(2,1)} %copy-done.1) | copy-start | bytes 1572868
  241.2 92.9 %all-reduce.2.cloned.1.call-start = ((), (), s32[]{:S(2)}) async-start(), calls=%async_computation.10 | async-start | bytes 2097152 | tf_op jit(solution)/shard_map/psum | solution.py:174
  248.5 1.7 copy-start.4
  250.0 304.6 %all-gather.2.cloned.1.call-start = ((), (), s32[]{:S(2)}) async-start(), calls=%async_computation.9 | async-start | bytes 28311552 | tf_op jit(solution)/shard_map/all_gather | solution.py:11
  317.4 2.5 copy-start.7
  327.3 0.9 copy-start.5
  327.3 252.6 %reduce-scatter.3.cloned.1.call-start = ((), (), s32[]{:S(2)}) async-start(), calls=%async_computation.7 | async-start | bytes 786432 | tf_op jit(solution)/shard_map/reduce_scatter | solution.py:165
  329.5 250.4 %reduce-scatter.5.cloned.1.call-start = ((), (), s32[]{:S(2)}) async-start(), calls=%async_computation.8 | async-start | bytes 786432 | tf_op jit(solution)/shard_map/reduce_scatter | solution.py:177
Sparse Core Ops, SparseCore 0:
  250.1 83.9 all-reduce.1
  335.7 218.8 all-gather.1
Sparse Core Ops, SparseCore 1:
  330.6 13.5 reduce-scatter.2
  346.9 14.5 reduce-scatter.4
